TPU v7x, 32 devices: a whole 2x2x4 slice. The times are simulated.
32 devices in a mesh: segment: 2 (over x), lat: 4 (over y, core), lon: 4 (over z).
Axes of the slice: x: 2, y: 2, z: 4, core: 2. Of those that a mesh axis runs over, the one named last changes fastest.
Arguments:
- segment_input: bfloat16 [2, 32, 256, 128], P('segment', 'lat', 'lon'), may hold values from -6 to 6
- weights: bfloat16 [2, 2, 3, 3, 128, 128], P('segment'), may hold values from -0.1875 to 0.1875
- biases: float32 [2, 2, 128], P('segment'), may hold values from -3 to 3
- out_grad: bfloat16 [2, 32, 256, 128], P('segment', 'lat', 'lon'), may hold values from -6 to 6
Outputs:
- weight_grad: float32 [2, 2, 3, 3, 128, 128], P('segment')
- bias_grad: float32 [2, 2, 128], P('segment')
- input_grad: bfloat16 [2, 32, 256, 128], P('segment', 'lat', 'lon')
- skip_grad: bfloat16 [2, 16, 128, 128], P('segment', 'lat', 'lon')
All inputs are finite; a program needn't handle non-finite values.
Results may differ from a plain program's by a relative error of at most 0.006.
Values may be sent and summed in bfloat16 or wider, within the bound.
A program may use at most 64 MiB of HBM per device.

v0:
```python
import functools
import math

import jax
import jax.numpy as jnp
from jax import lax
from jax.experimental import pallas as pl
from jax.experimental.pallas import tpu as pltpu
from jax.sharding import PartitionSpec as P

MESH = pl.DeviceIdType.MESH
F32 = jnp.float32
BF16 = jnp.bfloat16
PAD = 8
XROWS = 4
GROWS = 2
RELATIONS = ((1, 0), (-1, 0), (0, 1), (0, -1), (1, 1), (1, -1), (-1, 1), (-1, -1))


def triple(field, forward):
    count = field.shape[0]
    before = pltpu.roll(field, 1, 0).astype(BF16)
    after = pltpu.roll(field, count - 1, 0).astype(BF16)
    if forward:
        return before, field.astype(BF16), after
    return after, field.astype(BF16), before


def slope(value, sig):
    return sig * (1.0 + value * (1.0 - sig))


def kernel(sizes, x_hbm, w_hbm, b_ref, g_hbm,
           wout, bout, gin, skip,
           xin, gin_buf, wv, wt,
           xn, xs, xw, xe, xnw, xne, xsw, xse,
           gn, gs, gw, ge, gnw, gne, gsw, gse,
           x3, a3, g3, p3, s1,
           part, rc, m1, rl, mid, rn, bpart, bmid,
           pool32, pool, skip_in,
           local_sem, halo_send, halo_recv, red_send, red_recv, skip_send, skip_recv):
    nseg, L, N, H, W, C, S, used, scale = sizes
    WP, L2 = W + 2 * PAD, L // 2
    seg, lat, lon = lax.axis_index("segment"), lax.axis_index("lat"), lax.axis_index("lon")

    loads = [
        pltpu.make_async_copy(w_hbm, wv, local_sem.at[0]),
        pltpu.make_async_copy(x_hbm, xin, local_sem.at[1]),
        pltpu.make_async_copy(g_hbm, gin_buf, local_sem.at[2]),
    ]
    for load in loads:
        load.start()

    def lat_peer(d):
        return lax.rem(lat + d, L)

    def lon_peer(d):
        return lax.rem(lon + (d + N), N)

    barrier = pltpu.get_barrier_semaphore()

    def greet(s, a, o):
        pl.semaphore_signal(barrier, inc=1, device_id=(s, a, o), device_id_type=MESH)

    for d in range(1, L):
        greet(seg, lat_peer(d), lon)
    for d in range(1, N):
        greet(seg, lat, lon_peer(d))

    @pl.when(lat > 0)
    def _():
        greet(seg, lat - 1, lon_peer(1))
        greet(seg, lat - 1, lon_peer(-1))

    @pl.when(lat < L - 1)
    def _():
        greet(seg, lat + 1, lon_peer(1))
        greet(seg, lat + 1, lon_peer(-1))

    @pl.when(seg > 0)
    def _():
        greet(seg - 1, lat, lon)

    @pl.when(seg < nseg - 1)
    def _():
        greet(seg + 1, lat, lon)

    def flag(condition):
        return lax.convert_element_type(condition, jnp.int32)

    peers = (L - 1 + N - 1 + 2 * flag(lat > 0) + 2 * flag(lat < L - 1)
             + flag(seg > 0) + flag(seg < nseg - 1))
    pl.semaphore_wait(barrier, peers)

    xdst = {(1, 0): xn, (-1, 0): xs, (0, 1): xw, (0, -1): xe,
            (1, 1): xnw, (1, -1): xne, (-1, 1): xsw, (-1, -1): xse}
    gdst = {(1, 0): gn, (-1, 0): gs, (0, 1): gw, (0, -1): ge,
            (1, 1): gnw, (1, -1): gne, (-1, 1): gsw, (-1, -1): gse}

    def piece(ref, rows, dl, do):
        r = {1: pl.ds(H - rows, rows), -1: pl.ds(0, rows), 0: pl.ds(0, H)}[dl]
        c = {1: pl.ds(W - PAD, PAD), -1: pl.ds(0, PAD), 0: pl.ds(0, W)}[do]
        return ref.at[r, c]

    def halo_copy(which, k):
        dl, do = RELATIONS[k]
        ref, rows, dst = (x_hbm, XROWS, xdst) if which == 0 else (g_hbm, GROWS, gdst)
        at = which * len(RELATIONS) + k
        return pltpu.make_async_remote_copy(
            src_ref=piece(ref, rows, dl, do),
            dst_ref=dst[(dl, do)],
            send_sem=halo_send.at[at],
            recv_sem=halo_recv.at[at],
            device_id=(seg, lat + dl, lon_peer(do)),
            device_id_type=MESH,
        )

    def halo_each(which, act):
        for k, (dl, do) in enumerate(RELATIONS):
            if dl == 0:
                act(which, k, None)
            else:
                act(which, k, dl)

    def start_halo(which, k, dl):
        if dl is None:
            halo_copy(which, k).start()
        else:
            @pl.when((lat < L - 1) if dl == 1 else (lat > 0))
            def _():
                halo_copy(which, k).start()

    def recv_halo(which, k, dl):
        if dl is None:
            halo_copy(which, k).wait_recv()
        else:
            @pl.when((lat > 0) if dl == 1 else (lat < L - 1))
            def _():
                halo_copy(which, k).wait_recv()

    def sent_halo(which, k, dl):
        if dl is None:
            halo_copy(which, k).wait_send()
        else:
            @pl.when((lat < L - 1) if dl == 1 else (lat > 0))
            def _():
                halo_copy(which, k).wait_send()

    halo_each(0, start_halo)
    halo_each(1, start_halo)

    @pl.when(lat == 0)
    def _():
        for ref in (xn, xnw, xne, gn, gnw, gne):
            ref[...] = jnp.zeros(ref.shape, BF16)

    @pl.when(lat == L - 1)
    def _():
        for ref in (xs, xsw, xse, gs, gsw, gse):
            ref[...] = jnp.zeros(ref.shape, BF16)

    loads[0].wait()
    for ly in range(2):
        for k in range(9):
            wt[ly, k * C:(k + 1) * C, :] = wv[ly, k * C:(k + 1) * C, :].T
    loads[1].wait()
    loads[2].wait()
    halo_each(0, recv_halo)

    def assemble(n, nw, ne, mid_, w, e, s, sw, se):
        def band(a, b, c):
            return jnp.concatenate([a[...].astype(F32), b[...].astype(F32), c[...].astype(F32)], axis=1)
        whole = jnp.concatenate([band(nw, n, ne), band(w, mid_, e), band(sw, s, se)], axis=0)
        return whole.reshape(whole.shape[0] * WP, C)

    def put(ref, field, forward):
        for q, part_ in enumerate(triple(field, forward)):
            ref[:, q * C:(q + 1) * C] = part_

    def window(ref, starts, rows):
        return jnp.concatenate([ref[s * WP:(s + rows) * WP, :] for s in starts], axis=1)

    def clear(ref, first, rows, total):
        @pl.when(lat == 0)
        def _():
            ref[0:rows * WP, :] = jnp.zeros((rows * WP, 3 * C), BF16)

        @pl.when(lat == L - 1)
        def _():
            ref[(total - rows) * WP:total * WP, :] = jnp.zeros((rows * WP, 3 * C), BF16)

    put(x3, assemble(xn, xnw, xne, xin, xw, xe, xs, xsw, xse), True)
    R1, R2, R3 = H + 6, H + 4, H + 2
    z1 = jnp.dot(window(x3, (0, 1, 2), R1), wv[0], preferred_element_type=F32) + b_ref[0:1, :]
    sig = jax.nn.sigmoid(z1)
    s1[...] = slope(z1, sig)[2 * WP:(2 + R3) * WP, :]
    put(a3, z1 * sig, True)
    clear(a3, 0, 3, R1)

    halo_each(1, recv_halo)
    z2 = jnp.dot(window(a3, (0, 1, 2), R2), wv[1], preferred_element_type=F32) + b_ref[1:2, :]
    up = assemble(gn, gnw, gne, gin_buf, gw, ge, gs, gsw, gse)
    g2 = (up * slope(z2, jax.nn.sigmoid(z2)))
    put(g3, g2, False)

    column = lax.rem(lax.broadcasted_iota(jnp.int32, (H * WP, C), 0), WP)
    inside = (column >= PAD) & (column < PAD + W)

    def grads(field, start, first, ly, brow):
        own = jnp.where(inside, field[first * WP:(first + H) * WP, :].astype(BF16).astype(F32), 0.0)
        bsum = jnp.sum(own, axis=0, keepdims=True)
        bpart[lat, brow * 8:brow * 8 + 8, :] = jnp.broadcast_to(bsum, (8, C))
        flipped = own.astype(BF16).T
        ref = a3 if ly else x3
        for p in range(3):
            block = ref[(start + p) * WP:(start + p + H) * WP, :]
            three = jnp.dot(flipped, block, preferred_element_type=F32).astype(BF16)
            for q in range(3):
                yield three[:, q * C:(q + 1) * C].T

    def store_part(ly, blocks):
        whole = jnp.concatenate([v.astype(F32) for v in blocks], axis=0)
        extra = used * S - whole.shape[0]
        if extra:
            whole = jnp.concatenate([whole, jnp.zeros((extra, C), F32)], axis=0)
        for i in range(L * N):
            value = whole[i * S:(i + 1) * S].astype(BF16) if i < used else jnp.zeros((S, C), BF16)
            part[ly, i // (L2 * N), i // N % L2, i % N] = value

    def copy_to(src, dst, at, ly, peer):
        return pltpu.make_async_remote_copy(
            src_ref=src, dst_ref=dst, send_sem=red_send.at[ly, at], recv_sem=red_recv.at[ly, at],
            device_id=(seg,) + peer, device_id_type=MESH)

    def lat_copies(src_of, dst_of, base, ly):
        out, inc = [], []
        for d in range(1, L):
            to, frm = lat_peer(d), lat_peer(L - d)
            out.append(copy_to(src_of(to), dst_of(lat), base + d - 1, ly, (to, lon)))
            inc.append(copy_to(src_of(frm), dst_of(frm), base + d - 1, ly, (to, lon)))
        return out, inc

    def lon_copies(src_of, dst_of, base, ly):
        out, inc = [], []
        for d in range(1, N):
            to, frm = lon_peer(d), lon_peer(N - d)
            out.append(copy_to(src_of(to), dst_of(lon), base + d - 1, ly, (lat, to)))
            inc.append(copy_to(src_of(frm), dst_of(frm), base + d - 1, ly, (lat, to)))
        return out, inc

    pending = []

    def launch(pair):
        for c in pair[0]:
            c.start()
        pending.extend(pair[0])
        return pair[1]

    def arrive(incoming):
        for c in incoming:
            c.wait_recv()

    core, y = lax.rem(lat, 2), lat // 2
    partner = 2 * y + 1 - core

    def y_copies(src_of, dst_of, base, ly):
        out, inc = [], []
        for d in range(1, L2):
            to, frm = lax.rem(y + d, L2), lax.rem(y + L2 - d, L2)
            peer = (2 * to + core, lon)
            out.append(copy_to(src_of(to), dst_of(y), base + d - 1, ly, peer))
            inc.append(copy_to(src_of(frm), dst_of(frm), base + d - 1, ly, peer))
        return out, inc

    def y_slot(d):
        return lax.rem(y + d, L2)

    RSY, RSZ, AGZ, AGY, AGC = 1, 1 + L2, 1 + L2 + N, 1 + L2 + 2 * N, 1 + 2 * L2 + 2 * N

    def rs_core(ly):
        c = copy_to(part.at[ly, 1 - core], rc.at[ly], 0, ly, (partner, lon))
        return launch(([c], [c]))

    def rs_y(ly, incoming):
        arrive(incoming)
        m1[ly] = (part[ly, core].astype(F32) + rc[ly].astype(F32)).astype(BF16)
        return launch(y_copies(lambda to: m1.at[ly, to], lambda frm: rl.at[ly, frm], RSY, ly))

    def rs_lon(ly, incoming):
        arrive(incoming)
        total = m1[ly, y].astype(F32)
        for d in range(1, L2):
            total = total + rl[ly, y_slot(d)].astype(F32)
        mid[ly] = total.astype(BF16)
        return launch(lon_copies(lambda to: mid.at[ly, to], lambda frm: rn.at[ly, frm], RSZ, ly))

    def ag_lon(ly, incoming):
        arrive(incoming)
        total = mid[ly, lon].astype(F32)
        for d in range(1, N):
            total = total + rn[ly, lon_peer(d)].astype(F32)
        wout[ly, core, y, lon] = (total * scale).astype(BF16)
        return launch(lon_copies(lambda to: wout.at[ly, core, y, lon],
                                 lambda frm: wout.at[ly, core, y, frm], AGZ, ly))

    def core_copy(ly, d):
        out = copy_to(wout.at[ly, core, y_slot(d)], wout.at[ly, core, y_slot(d)], AGC + d, ly, (partner, lon))
        inc = copy_to(wout.at[ly, core, y_slot(d)], wout.at[ly, 1 - core, y_slot(d)], AGC + d, ly, (partner, lon))
        return [out], [inc]

    def ag_y(ly, incoming):
        arrive(incoming)
        other = launch(y_copies(lambda to: wout.at[ly, core, y], lambda frm: wout.at[ly, core, frm], AGY, ly))
        return other, launch(core_copy(ly, 0))

    def ag_core(ly, incoming):
        others, last = incoming
        for d in range(1, L2):
            arrive([others[L2 - d - 1]])
            last = last + launch(core_copy(ly, d))
        return last

    store_part(1, grads(g2, 2, 2, 1, 1))
    inc2 = rs_core(1)

    h1 = lax.dot_general(window(g3, (2, 1, 0), R3), wt[1], (((1,), (0,)), ((), ())),
                         preferred_element_type=F32)
    g1 = h1 * s1[...]
    put(p3, g1, False)
    clear(p3, 0, 1, R3)
    inc2 = rs_y(1, inc2)

    store_part(0, grads(g1, 3, 1, 0, 0))
    inc1 = rs_core(0)
    binc = launch(lat_copies(lambda to: bpart.at[lat], lambda frm: bpart.at[frm], 0, 2))
    inc1 = rs_y(0, inc1)
    inc2 = rs_lon(1, inc2)

    gi = jnp.dot(window(p3, (2, 1, 0), H), wt[0], preferred_element_type=F32)
    gi = gi.reshape(H, WP, C)[:, PAD:PAD + W, :]
    gin[...] = gi.astype(BF16)
    rows = gi.reshape(H // 2, 2, W, C)
    pool32[...] = (rows[:, 0] + rows[:, 1]).reshape(H // 2 * W, C)
    half = H // 2 * W // 2
    pool[...] = (pool32[pl.ds(0, half, stride=2), :] + pool32[pl.ds(1, half, stride=2), :]).astype(BF16)

    def skip_copy(to):
        return pltpu.make_async_remote_copy(
            src_ref=pool, dst_ref=skip_in, send_sem=skip_send, recv_sem=skip_recv,
            device_id=(to, lat, lon), device_id_type=MESH)

    @pl.when(seg > 0)
    def _():
        skip_copy(seg - 1).start()

    inc1 = rs_lon(0, inc1)
    inc2 = ag_lon(1, inc2)
    arrive(binc)
    total = bpart[0]
    for i in range(1, L):
        total = total + bpart[i]
    bmid[lon] = total
    binc = launch(lon_copies(lambda to: bmid.at[lon], lambda frm: bmid.at[frm], L, 2))
    inc1 = ag_lon(0, inc1)
    inc2 = ag_y(1, inc2)
    inc1 = ag_y(0, inc1)
    inc2 = ag_core(1, inc2)
    inc1 = ag_core(0, inc1)
    arrive(binc)
    total = bmid[0]
    for i in range(1, N):
        total = total + bmid[i]
    bout[...] = jnp.concatenate([total[0:1], total[8:9]], axis=0) * scale

    @pl.when(seg < nseg - 1)
    def _():
        skip_copy(seg).wait_recv()
        skip[...] = skip_in[...]

    @pl.when(seg == nseg - 1)
    def _():
        skip[...] = jnp.zeros(skip.shape, BF16)

    arrive(inc2)
    arrive(inc1)
    for c in pending:
        c.wait_send()
    halo_each(0, sent_halo)
    halo_each(1, sent_halo)

    @pl.when(seg > 0)
    def _():
        skip_copy(seg - 1).wait_send()


def body(mesh_sizes, segment_input, weights, biases, out_grad):
    nseg, L, N = mesh_sizes
    _, H, W, C = segment_input.shape
    total_rows = 9 * C
    S = 8 * (-(-total_rows // (8 * L * N)))
    used = -(-total_rows // S)
    scale = 1.0 / math.sqrt(H * L * W * N)
    WP = W + 2 * PAD
    sizes = (nseg, L, N, H, W, C, S, used, scale)
    VM = pltpu.VMEM
    halos = []
    for rows in (XROWS, GROWS):
        halos += [VM((rows, W, C), BF16)] * 2 + [VM((H, PAD, C), BF16)] * 2 + [VM((rows, PAD, C), BF16)] * 4
    dma = pltpu.SemaphoreType.DMA
    per = 2 * (L + N) + 2
    vmem = pl.BlockSpec(memory_space=pltpu.VMEM)
    anyspace = pl.BlockSpec(memory_space=pl.ANY)
    wout, bout, gin, skip = pl.pallas_call(
        functools.partial(kernel, sizes),
        out_shape=(
            jax.ShapeDtypeStruct((2, 2, L // 2, N, S, C), BF16),
            jax.ShapeDtypeStruct((2, C), F32),
            jax.ShapeDtypeStruct((H, W, C), BF16),
            jax.ShapeDtypeStruct((H // 2 * W // 2, C), BF16),
        ),
        in_specs=[anyspace, anyspace, vmem, anyspace],
        out_specs=(vmem, vmem, vmem, vmem),
        scratch_shapes=[
            VM((H, W, C), BF16), VM((H, W, C), BF16),
            VM((2, 9 * C, C), BF16), VM((2, 9 * C, C), BF16),
            *halos,
            VM(((H + 8) * WP, 3 * C), BF16), VM(((H + 6) * WP, 3 * C), BF16),
            VM(((H + 4) * WP, 3 * C), BF16), VM(((H + 2) * WP, 3 * C), BF16),
            VM(((H + 2) * WP, C), F32),
            VM((2, 2, L // 2, N, S, C), BF16), *[VM((2, L // 2, N, S, C), BF16)] * 3,
            VM((2, N, S, C), BF16), VM((2, N, S, C), BF16),
            VM((L, 16, C), F32), VM((N, 16, C), F32),
            VM((H // 2 * W, C), F32), VM((H // 2 * W // 2, C), BF16), VM((H // 2 * W // 2, C), BF16),
            dma((3,)), dma((16,)), dma((16,)), dma((3, per)), dma((3, per)), dma(()), dma(()),
        ],
        compiler_params=pltpu.CompilerParams(collective_id=0, has_side_effects=True),
    )(segment_input[0], weights[0].reshape(2, 9 * C, C), biases[0], out_grad[0])
    flat = wout.reshape(2, L * N * S, C)[:, :total_rows]
    weight_grad = flat.astype(F32).reshape(1, 2, 3, 3, C, C)
    bias_grad = bout[None]
    return weight_grad, bias_grad, gin[None], skip.reshape(1, H // 2, W // 2, C)


def solution(mesh):
    placed = (
        P("segment", "lat", "lon", None),
        P("segment", None, None, None, None, None),
        P("segment", None, None),
        P("segment", "lat", "lon", None),
    )
    mesh_sizes = (mesh.shape["segment"], mesh.shape["lat"], mesh.shape["lon"])
    return jax.shard_map(
        functools.partial(body, mesh_sizes),
        mesh=mesh,
        in_specs=placed,
        out_specs=(
            P("segment", None, None, None, None, None),
            P("segment", None, None),
            P("segment", "lat", "lon", None),
            P("segment", "lat", "lon", None),
        ),
        check_vma=False,
    )
```

profile of v0, /device:TPU:0, one launch (start us, length us, event | category | flops | bytes accessed | tf_op | source)
XLA Modules:
  0.0 39.5 jit_solution(16054132802709827265)
XLA Ops:
  0.6 34.8 %shard_map.75 = (bf16[2,2,2,4,72,128]{5,4,3,2,1,0:T(8,128)(2,1)}, f32[2,128]{1,0:T(2,128)}, bf16[8,64,128]{2,1,0:T(8,128)(2,1)}, bf16[128,128]{1,0:T(8,128)(2,1)}) custom-call(bf16[8,64,128]{2,1,0:T(8,128)(2,1)} %bitcast.12, bf16[2,1152,128]{2,1,0:T(8,128)(2,1)} %bitcast.10, f32[2,128]{1,0:T(2,128)} %bitcast.15, bf16[8,64,128]{2,1,0:T(8,128)(2,1)} %bitcast.13), custom_call_target="tpu_custom_call" | custom-call | tf_op jit(solution)/shard_map/pallas_call | solution.py:413
  35.4 0.0 copy-start.2
  35.4 0.0 copy-start
  35.4 0.0 copy-start.1
  35.4 2.2 %convert.1 = f32[1,2,3,3,128,128]{5,4,3,2,1,0:T(8,128)} convert(bf16[1,2,3,3,128,128]{5,4,3,2,1,0:T(8,128)(2,1)} %bitcast.9) | non-fusion elementwise | flops 294912 | bytes 1769472 | tf_op jit(solution)/shard_map/convert_element_type | solution.py:439
  37.7 0.0 copy-done.2
  37.7 0.6 %copy.11 = f32[1,2,128]{2,1,0:T(2,128)} copy(f32[1,2,128]{2,1,0:T(2,128)S(1)} %bitcast.16) | data formatting | bytes 2048
  38.2 0.0 copy-done
  38.2 0.7 %copy.12 = bf16[1,8,64,128]{3,2,1,0:T(8,128)(2,1)} copy(bf16[1,8,64,128]{3,2,1,0:T(8,128)(2,1)S(1)} %bitcast.11) | data formatting | bytes 262144
  38.9 0.0 copy-done.1
  38.9 0.6 %copy.13 = bf16[1,4,32,128]{3,2,1,0:T(8,128)(2,1)} copy(bf16[1,4,32,128]{3,2,1,0:T(8,128)(2,1)S(1)} %bitcast.14) | data formatting | bytes 65536
Async XLA Ops:
  35.4 2.3 %copy-start.2 = (f32[2,128]{1,0:T(2,128)S(1)}, f32[2,128]{1,0:T(2,128)}, u32[]{:S(2)}) copy-start(f32[2,128]{1,0:T(2,128)} %get-tuple-element.9) | copy-start | bytes 3076
  35.4 2.8 %copy-start = (bf16[8,64,128]{2,1,0:T(8,128)(2,1)S(1)}, bf16[8,64,128]{2,1,0:T(8,128)(2,1)}, u32[]{:S(2)}) copy-start(bf16[8,64,128]{2,1,0:T(8,128)(2,1)} %get-tuple-element.10) | copy-start | bytes 393220
  35.4 3.5 %copy-start.1 = (bf16[128,128]{1,0:T(8,128)(2,1)S(1)}, bf16[128,128]{1,0:T(8,128)(2,1)}, u32[]{:S(2)}) copy-start(bf16[128,128]{1,0:T(8,128)(2,1)} %get-tuple-element.11) | copy-start | bytes 98308
where the time goes:
time: 39.7 us; the launch traced here: 39.5 us
  Pallas kernels  34.8 us (88%)
  other arithmetic  2.24 us (6%)
  local copies, waits for them, and re-layouts  1.84 us (5%)
  between operations  0.67 us (2%)
    pallas_call x1, Pallas kernels, body(): pl.pallas_call(functools.partial(kernel, sizes), out_shape=(jax.ShapeDtyp...  34.8 us
    convert_element_type x1, other arithmetic, body(): weight_grad = flat.astype(F32).reshape(1, 2, 3, 3, C, C)  2.24 us
    unnamed x9, local copies, waits for them, and re-layouts  1.84 us

commit v1 on v0

--- a/solution.py
+++ b/solution.py
@@ -30,9 +30,9 @@
     return sig * (1.0 + value * (1.0 - sig))
 
 
-def kernel(sizes, x_hbm, w_hbm, b_ref, g_hbm,
+def kernel(sizes, x_hbm, w_hbm, b_hbm, g_hbm,
            wout, bout, gin, skip,
-           xin, gin_buf, wv, wt,
+           xin, gin_buf, b_ref, wv, wt,
            xn, xs, xw, xe, xnw, xne, xsw, xse,
            gn, gs, gw, ge, gnw, gne, gsw, gse,
            x3, a3, g3, p3, s1,
@@ -47,6 +47,7 @@
         pltpu.make_async_copy(w_hbm, wv, local_sem.at[0]),
         pltpu.make_async_copy(x_hbm, xin, local_sem.at[1]),
         pltpu.make_async_copy(g_hbm, gin_buf, local_sem.at[2]),
+        pltpu.make_async_copy(b_hbm, b_ref, local_sem.at[3]),
     ]
     for load in loads:
         load.start()
@@ -165,6 +166,7 @@
             wt[ly, k * C:(k + 1) * C, :] = wv[ly, k * C:(k + 1) * C, :].T
     loads[1].wait()
     loads[2].wait()
+    loads[3].wait()
     halo_each(0, recv_halo)
 
     def assemble(n, nw, ne, mid_, w, e, s, sw, se):
@@ -393,6 +395,22 @@
         skip_copy(seg - 1).wait_send()
 
 
+def finish(rows, w_ref, b_ref, gin_ref, skip_ref, w_out, b_out, gin_out, skip_out, wide, sem):
+    copies = [pltpu.make_async_copy(gin_ref, gin_out, sem.at[0]),
+              pltpu.make_async_copy(b_ref, b_out, sem.at[1]),
+              pltpu.make_async_copy(skip_ref, skip_out, sem.at[2])]
+    for copy in copies:
+        copy.start()
+    for ly in range(2):
+        flat = w_ref[ly].reshape(-1, w_ref.shape[-1])
+        wide[ly] = flat[:rows].astype(F32)
+        copy = pltpu.make_async_copy(wide.at[ly], w_out.at[ly], sem.at[3 + ly])
+        copy.start()
+        copies.append(copy)
+    for copy in copies:
+        copy.wait()
+
+
 def body(mesh_sizes, segment_input, weights, biases, out_grad):
     nseg, L, N = mesh_sizes
     _, H, W, C = segment_input.shape
@@ -410,18 +428,25 @@
     per = 2 * (L + N) + 2
     vmem = pl.BlockSpec(memory_space=pltpu.VMEM)
     anyspace = pl.BlockSpec(memory_space=pl.ANY)
+    hbm = pl.BlockSpec(memory_space=pltpu.HBM)
+    half = H // 2 * W // 2
+    finish_bytes = 2 * total_rows * C * 4 + (1 << 20)
+
+    def in_hbm(array):
+        return pltpu.with_memory_space_constraint(array, pltpu.HBM)
+
     wout, bout, gin, skip = pl.pallas_call(
         functools.partial(kernel, sizes),
         out_shape=(
-            jax.ShapeDtypeStruct((2, 2, L // 2, N, S, C), BF16),
-            jax.ShapeDtypeStruct((2, C), F32),
-            jax.ShapeDtypeStruct((H, W, C), BF16),
-            jax.ShapeDtypeStruct((H // 2 * W // 2, C), BF16),
+            VM((2, 2, L // 2, N, S, C), BF16),
+            VM((2, C), F32),
+            VM((H, W, C), BF16),
+            VM((half, C), BF16),
         ),
-        in_specs=[anyspace, anyspace, vmem, anyspace],
+        in_specs=[hbm, hbm, hbm, hbm],
         out_specs=(vmem, vmem, vmem, vmem),
         scratch_shapes=[
-            VM((H, W, C), BF16), VM((H, W, C), BF16),
+            VM((H, W, C), BF16), VM((H, W, C), BF16), VM((2, C), F32),
             VM((2, 9 * C, C), BF16), VM((2, 9 * C, C), BF16),
             *halos,
             VM(((H + 8) * WP, 3 * C), BF16), VM(((H + 6) * WP, 3 * C), BF16),
@@ -431,14 +456,26 @@
             VM((2, N, S, C), BF16), VM((2, N, S, C), BF16),
             VM((L, 16, C), F32), VM((N, 16, C), F32),
             VM((H // 2 * W, C), F32), VM((H // 2 * W // 2, C), BF16), VM((H // 2 * W // 2, C), BF16),
-            dma((3,)), dma((16,)), dma((16,)), dma((3, per)), dma((3, per)), dma(()), dma(()),
+            dma((4,)), dma((16,)), dma((16,)), dma((3, per)), dma((3, per)), dma(()), dma(()),
         ],
-        compiler_params=pltpu.CompilerParams(collective_id=0, has_side_effects=True),
-    )(segment_input[0], weights[0].reshape(2, 9 * C, C), biases[0], out_grad[0])
-    flat = wout.reshape(2, L * N * S, C)[:, :total_rows]
-    weight_grad = flat.astype(F32).reshape(1, 2, 3, 3, C, C)
-    bias_grad = bout[None]
-    return weight_grad, bias_grad, gin[None], skip.reshape(1, H // 2, W // 2, C)
+        compiler_params=pltpu.CompilerParams(collective_id=0, has_side_effects=True,
+                                             vmem_limit_bytes=48 << 20),
+    )(in_hbm(segment_input[0]), in_hbm(weights[0].reshape(2, 9 * C, C)), in_hbm(biases[0]), in_hbm(out_grad[0]))
+    weight_grad, bias_grad, gin, skip = pl.pallas_call(
+        functools.partial(finish, total_rows),
+        out_shape=(
+            jax.ShapeDtypeStruct((2, total_rows, C), F32),
+            jax.ShapeDtypeStruct((2, C), F32),
+            jax.ShapeDtypeStruct((H, W, C), BF16),
+            jax.ShapeDtypeStruct((half, C), BF16),
+        ),
+        in_specs=[vmem] * 4,
+        out_specs=(anyspace,) * 4,
+        scratch_shapes=[VM((2, total_rows, C), F32), dma((5,))],
+        compiler_params=pltpu.CompilerParams(vmem_limit_bytes=finish_bytes),
+    )(wout, bout, gin, skip)
+    return (weight_grad.reshape(1, 2, 3, 3, C, C), bias_grad[None], gin[None],
+            skip.reshape(1, H // 2, W // 2, C))
 
 
 def solution(mesh):

time: 39.7 us -> 35.2 us (0.89)
  other arithmetic: 2.24 us -> 0 us
  local copies, waits for them, and re-layouts: 1.84 us -> 0 us
  Pallas kernels: 34.8 us -> 34.4 us
    convert_element_type x1 -> x0, other arithmetic: 2.24 us -> none  [body(): weight_grad = flat.astype(F32).reshape(1, 2, 3, 3, C, C)]
    unnamed x9 -> x0, local copies, waits for them, and re-layouts: 1.84 us -> none
    pallas_call x1 -> x2, Pallas kernels: 34.8 us -> 34.4 us  [the longest x1 33.3 us: body(): pl.pallas_call(functools.partial(kernel, sizes), out_shape=(VM((2, 2, L /...]
where the time goes in v1:
time: 35.2 us; the launch traced here: 35.1 us
  Pallas kernels  34.4 us (98%)
  between operations  0.64 us (2%)
    pallas_call x1, Pallas kernels, body(): pl.pallas_call(functools.partial(kernel, sizes), out_shape=(VM((2, 2, L /...  33.3 us
    pallas_call x1, Pallas kernels, body(): pl.pallas_call(functools.partial(finish, total_rows), out_shape=(jax.Shap...  1.11 us

profile of v1, /device:TPU:0, one launch (start us, length us, event | category | flops | bytes accessed | tf_op | source)
XLA Modules:
  0.0 35.1 jit_solution(4348335607801384911)
XLA Ops:
  0.6 33.3 %shard_map.75 = (bf16[2,2,2,4,72,128]{5,4,3,2,1,0:T(8,128)(2,1)S(1)}, f32[2,128]{1,0:T(2,128)S(1)}, bf16[8,64,128]{2,1,0:T(8,128)(2,1)S(1)}, bf16[128,128]{1,0:T(8,128)(2,1)S(1)}) custom-call(bf16[8,64,128]{2,1,0:T(8,128)(2,1)} %bitcast.9, bf16[2,1152,128]{2,1,0:T(8,128)(2,1)} %bitcast.8, f32[2,128]{1,0:T(2,128)} %bitcast.11, bf16[8,64,128]{2,1,0:T(8,128)(2,1)} %bitcast.10), custom_call_target="tpu_custom_call" | custom-call | tf_op jit(solution)/shard_map/pallas_call | solution.py:438
  34.0 1.1 %shard_map.76 = (f32[2,1152,128]{2,1,0:T(8,128)}, f32[2,128]{1,0:T(2,128)}, bf16[8,64,128]{2,1,0:T(8,128)(2,1)}, bf16[128,128]{1,0:T(8,128)(2,1)}) custom-call(bf16[2,2,2,4,72,128]{5,4,3,2,1,0:T(8,128)(2,1)S(1)} %get-tuple-element.12.w_ref, f32[2,128]{1,0:T(2,128)S(1)} %get-tuple-element.13.b_ref, bf16[8,64,128]{2,1,0:T(8,128)(2,1)S(1)} %get-tuple-element.14.gin_ref, ...), custom_call_target="tpu_custom_call" | custom-call | tf_op jit(solution)/shard_map/pallas_call | solution.py:464

commit v2 on v1

--- a/solution.py
+++ b/solution.py
@@ -14,6 +14,7 @@
 PAD = 8
 XROWS = 4
 GROWS = 2
+GROUPS = 4
 RELATIONS = ((1, 0), (-1, 0), (0, 1), (0, -1), (1, 1), (1, -1), (-1, 1), (-1, -1))
 
 
@@ -39,7 +40,7 @@
            part, rc, m1, rl, mid, rn, bpart, bmid,
            pool32, pool, skip_in,
            local_sem, halo_send, halo_recv, red_send, red_recv, skip_send, skip_recv):
-    nseg, L, N, H, W, C, S, used, scale = sizes
+    nseg, L, N, H, W, C, S, used, scale, G = sizes
     WP, L2 = W + 2 * PAD, L // 2
     seg, lat, lon = lax.axis_index("segment"), lax.axis_index("lat"), lax.axis_index("lon")
 
@@ -263,80 +264,133 @@
             c.wait_recv()
 
     core, y = lax.rem(lat, 2), lat // 2
-    partner = 2 * y + 1 - core
-
-    def y_copies(src_of, dst_of, base, ly):
-        out, inc = [], []
+    partner = (2 * y + 1 - core, lon)
+    Z = N // G
+    own = lon // Z
+    low = 2 * lon < N
+    mirrored = jnp.where(low, own, G - 1 - own)
+
+    def near(k):
+        if k == 0:
+            return own
+        at = k - 1 + jnp.where(k - 1 >= mirrored, 1, 0)
+        return jnp.where(low, at, G - 1 - at)
+
+    def zs(k):
+        return pl.ds(near(k) * Z, Z)
+
+    def y_to(d):
+        return lax.rem(y + d, L2)
+
+    def y_peer(d):
+        return (2 * y_to(d) + core, lon)
+
+    CRS, YRS = 0, G
+    ZRS = YRS + (L2 - 1) * G
+    ZAG = ZRS + N
+    YAG = ZAG + N
+    CAG = YAG + (L2 - 1) * G
+
+    def send(src, dst, at, ly, peer):
+        c = copy_to(src, dst, at, ly, peer)
+        c.start()
+        pending.append(c)
+
+    def rs_core(ly):
+        for k in reversed(range(G)):
+            send(part.at[ly, 1 - core, :, zs(k)], rc.at[ly, :, zs(k)], CRS + k, ly, partner)
+
+    def rs_y(ly, k):
+        copy_to(part.at[ly, 1 - core, :, zs(k)], rc.at[ly, :, zs(k)], CRS + k, ly, partner).wait_recv()
+        m1[ly, :, zs(k)] = (part[ly, core, :, zs(k)].astype(F32) + rc[ly, :, zs(k)].astype(F32)).astype(BF16)
         for d in range(1, L2):
-            to, frm = lax.rem(y + d, L2), lax.rem(y + L2 - d, L2)
-            peer = (2 * to + core, lon)
-            out.append(copy_to(src_of(to), dst_of(y), base + d - 1, ly, peer))
-            inc.append(copy_to(src_of(frm), dst_of(frm), base + d - 1, ly, peer))
-        return out, inc
-
-    def y_slot(d):
-        return lax.rem(y + d, L2)
-
-    RSY, RSZ, AGZ, AGY, AGC = 1, 1 + L2, 1 + L2 + N, 1 + L2 + 2 * N, 1 + 2 * L2 + 2 * N
-
-    def rs_core(ly):
-        c = copy_to(part.at[ly, 1 - core], rc.at[ly], 0, ly, (partner, lon))
-        return launch(([c], [c]))
-
-    def rs_y(ly, incoming):
-        arrive(incoming)
-        m1[ly] = (part[ly, core].astype(F32) + rc[ly].astype(F32)).astype(BF16)
-        return launch(y_copies(lambda to: m1.at[ly, to], lambda frm: rl.at[ly, frm], RSY, ly))
-
-    def rs_lon(ly, incoming):
-        arrive(incoming)
-        total = m1[ly, y].astype(F32)
-        for d in range(1, L2):
-            total = total + rl[ly, y_slot(d)].astype(F32)
-        mid[ly] = total.astype(BF16)
-        return launch(lon_copies(lambda to: mid.at[ly, to], lambda frm: rn.at[ly, frm], RSZ, ly))
-
-    def ag_lon(ly, incoming):
-        arrive(incoming)
+            send(m1.at[ly, y_to(d), zs(k)], rl.at[ly, y, zs(k)], YRS + (d - 1) * G + k, ly, y_peer(d))
+
+    def z_far(base, src_of, dst, ly, k, away):
+        for j in reversed(range(Z)):
+            t = near(k) * Z + j
+            away(t, copy_to(src_of(t), dst, base + lax.rem(t - lon + N, N), ly, (lat, t)))
+
+    def z_start(t, c):
+        @pl.when(t != lon)
+        def _():
+            c.start()
+
+    def z_sent(t, c):
+        @pl.when(t != lon)
+        def _():
+            c.wait_send()
+
+    def rs_z(ly, k, act=z_start):
+        if act is z_start:
+            total = m1[ly, y, zs(k)].astype(F32)
+            for d in range(1, L2):
+                frm = y_to(L2 - d)
+                copy_to(m1.at[ly, frm, zs(k)], rl.at[ly, frm, zs(k)], YRS + (d - 1) * G + k, ly,
+                        y_peer(d)).wait_recv()
+                total = total + rl[ly, frm, zs(k)].astype(F32)
+            mid[ly, zs(k)] = total.astype(BF16)
+        z_far(ZRS, lambda t: mid.at[ly, t], rn.at[ly, lon], ly, k, act)
+
+    def z_wait(src, dst_of, base, ly, frm):
+        copy_to(src, dst_of(frm), base + lax.rem(lon - frm + N, N), ly, (lat, frm)).wait_recv()
+
+    def total_z(ly):
         total = mid[ly, lon].astype(F32)
+        for d in range(1, N):
+            frm = lon_peer(d)
+            z_wait(mid.at[ly, frm], lambda i: rn.at[ly, i], ZRS, ly, frm)
         for d in range(1, N):
             total = total + rn[ly, lon_peer(d)].astype(F32)
         wout[ly, core, y, lon] = (total * scale).astype(BF16)
-        return launch(lon_copies(lambda to: wout.at[ly, core, y, lon],
-                                 lambda frm: wout.at[ly, core, y, frm], AGZ, ly))
-
-    def core_copy(ly, d):
-        out = copy_to(wout.at[ly, core, y_slot(d)], wout.at[ly, core, y_slot(d)], AGC + d, ly, (partner, lon))
-        inc = copy_to(wout.at[ly, core, y_slot(d)], wout.at[ly, 1 - core, y_slot(d)], AGC + d, ly, (partner, lon))
-        return [out], [inc]
-
-    def ag_y(ly, incoming):
-        arrive(incoming)
-        other = launch(y_copies(lambda to: wout.at[ly, core, y], lambda frm: wout.at[ly, core, frm], AGY, ly))
-        return other, launch(core_copy(ly, 0))
-
-    def ag_core(ly, incoming):
-        others, last = incoming
+        for k in reversed(range(G)):
+            ag_z(ly, k, z_start)
+
+    def ag_z(ly, k, act):
+        z_far(ZAG, lambda t: wout.at[ly, core, y, lon], wout.at[ly, core, y, lon], ly, k, act)
+
+    def forward(ly, k):
+        for j in range(Z):
+            frm = near(k) * Z + j
+
+            @pl.when(frm != lon)
+            def _():
+                z_wait(wout.at[ly, core, y, lon], lambda i: wout.at[ly, core, y, i], ZAG, ly, frm)
+
+        piece = wout.at[ly, core, y, zs(k)]
         for d in range(1, L2):
-            arrive([others[L2 - d - 1]])
-            last = last + launch(core_copy(ly, d))
-        return last
+            send(piece, piece, YAG + (d - 1) * G + k, ly, y_peer(d))
+        send(piece, piece, CAG + k, ly, partner)
+
+    def forward_y(ly, k):
+        for d in range(1, L2):
+            piece = wout.at[ly, core, y_to(L2 - d), zs(k)]
+            copy_to(wout.at[ly, core, y, zs(k)], piece, YAG + (d - 1) * G + k, ly, y_peer(d)).wait_recv()
+            send(piece, piece, CAG + d * G + k, ly, partner)
+
+    def settle(ly):
+        for k in range(G):
+            for d in range(L2):
+                at = y_to(L2 - d) if d else y
+                copy_to(wout.at[ly, core, at, zs(k)], wout.at[ly, 1 - core, at, zs(k)], CAG + d * G + k, ly,
+                        partner).wait_recv()
+            rs_z(ly, k, z_sent)
+            ag_z(ly, k, z_sent)
 
     store_part(1, grads(g2, 2, 2, 1, 1))
-    inc2 = rs_core(1)
+    rs_core(1)
 
     h1 = lax.dot_general(window(g3, (2, 1, 0), R3), wt[1], (((1,), (0,)), ((), ())),
                          preferred_element_type=F32)
     g1 = h1 * s1[...]
     put(p3, g1, False)
     clear(p3, 0, 1, R3)
-    inc2 = rs_y(1, inc2)
+    for k in reversed(range(G)):
+        rs_y(1, k)
 
     store_part(0, grads(g1, 3, 1, 0, 0))
-    inc1 = rs_core(0)
+    rs_core(0)
     binc = launch(lat_copies(lambda to: bpart.at[lat], lambda frm: bpart.at[frm], 0, 2))
-    inc1 = rs_y(0, inc1)
-    inc2 = rs_lon(1, inc2)
 
     gi = jnp.dot(window(p3, (2, 1, 0), H), wt[0], preferred_element_type=F32)
     gi = gi.reshape(H, WP, C)[:, PAD:PAD + W, :]
@@ -351,23 +405,34 @@
             src_ref=pool, dst_ref=skip_in, send_sem=skip_send, recv_sem=skip_recv,
             device_id=(to, lat, lon), device_id_type=MESH)
 
+    for k in reversed(range(G)):
+        rs_y(0, k)
+
     @pl.when(seg > 0)
     def _():
         skip_copy(seg - 1).start()
 
-    inc1 = rs_lon(0, inc1)
-    inc2 = ag_lon(1, inc2)
+    for k in reversed(range(G)):
+        rs_z(1, k)
     arrive(binc)
     total = bpart[0]
     for i in range(1, L):
         total = total + bpart[i]
     bmid[lon] = total
     binc = launch(lon_copies(lambda to: bmid.at[lon], lambda frm: bmid.at[frm], L, 2))
-    inc1 = ag_lon(0, inc1)
-    inc2 = ag_y(1, inc2)
-    inc1 = ag_y(0, inc1)
-    inc2 = ag_core(1, inc2)
-    inc1 = ag_core(0, inc1)
+    for k in reversed(range(G)):
+        rs_z(0, k)
+    total_z(1)
+    for k in range(G - 2):
+        forward(1, k)
+    total_z(0)
+    forward(0, 0)
+    for k in range(G - 2, G):
+        forward(1, k)
+    for k in range(G):
+        forward_y(1, k)
+    for k in range(1, G):
+        forward(0, k)
     arrive(binc)
     total = bmid[0]
     for i in range(1, N):
@@ -383,8 +448,10 @@
     def _():
         skip[...] = jnp.zeros(skip.shape, BF16)
 
-    arrive(inc2)
-    arrive(inc1)
+    for k in range(G):
+        forward_y(0, k)
+    settle(1)
+    settle(0)
     for c in pending:
         c.wait_send()
     halo_each(0, sent_halo)
@@ -419,13 +486,14 @@
     used = -(-total_rows // S)
     scale = 1.0 / math.sqrt(H * L * W * N)
     WP = W + 2 * PAD
-    sizes = (nseg, L, N, H, W, C, S, used, scale)
+    G = math.gcd(N, GROUPS)
+    sizes = (nseg, L, N, H, W, C, S, used, scale, G)
     VM = pltpu.VMEM
     halos = []
     for rows in (XROWS, GROWS):
         halos += [VM((rows, W, C), BF16)] * 2 + [VM((H, PAD, C), BF16)] * 2 + [VM((rows, PAD, C), BF16)] * 4
     dma = pltpu.SemaphoreType.DMA
-    per = 2 * (L + N) + 2
+    per = max(L + N, G * (1 + 2 * (L // 2 - 1) + L // 2) + 2 * N)
     vmem = pl.BlockSpec(memory_space=pltpu.VMEM)
     anyspace = pl.BlockSpec(memory_space=pl.ANY)
     hbm = pl.BlockSpec(memory_space=pltpu.HBM)

time: 35.2 us -> 36 us (1.023)
  Pallas kernels: 34.4 us -> 35.2 us
    pallas_call x1, Pallas kernels: 33.3 us -> 34.1 us  [body(): pl.pallas_call(functools.partial(kernel, sizes), out_shape=(VM((2, 2, L /...]
where the time goes in v2:
time: 36 us; the launch traced here: 35.9 us
  Pallas kernels  35.2 us (98%)
  between operations  0.64 us (2%)
    pallas_call x1, Pallas kernels, body(): pl.pallas_call(functools.partial(kernel, sizes), out_shape=(VM((2, 2, L /...  34.1 us
    pallas_call x1, Pallas kernels, body(): pl.pallas_call(functools.partial(finish, total_rows), out_shape=(jax.Shap...  1.11 us

profile of v2, /device:TPU:0, one launch (start us, length us, event | category | flops | bytes accessed | tf_op | source)
XLA Modules:
  0.0 35.9 jit_solution(2618012216886846920)
XLA Ops:
  0.6 34.1 %shard_map.75 = (bf16[2,2,2,4,72,128]{5,4,3,2,1,0:T(8,128)(2,1)S(1)}, f32[2,128]{1,0:T(2,128)S(1)}, bf16[8,64,128]{2,1,0:T(8,128)(2,1)S(1)}, bf16[128,128]{1,0:T(8,128)(2,1)S(1)}) custom-call(bf16[8,64,128]{2,1,0:T(8,128)(2,1)} %bitcast.9, bf16[2,1152,128]{2,1,0:T(8,128)(2,1)} %bitcast.8, f32[2,128]{1,0:T(2,128)} %bitcast.11, bf16[8,64,128]{2,1,0:T(8,128)(2,1)} %bitcast.10), custom_call_target="tpu_custom_call" | custom-call | tf_op jit(solution)/shard_map/pallas_call | solution.py:506
  34.8 1.1 %shard_map.76 = (f32[2,1152,128]{2,1,0:T(8,128)}, f32[2,128]{1,0:T(2,128)}, bf16[8,64,128]{2,1,0:T(8,128)(2,1)}, bf16[128,128]{1,0:T(8,128)(2,1)}) custom-call(bf16[2,2,2,4,72,128]{5,4,3,2,1,0:T(8,128)(2,1)S(1)} %get-tuple-element.12.w_ref, f32[2,128]{1,0:T(2,128)S(1)} %get-tuple-element.13.b_ref, bf16[8,64,128]{2,1,0:T(8,128)(2,1)S(1)} %get-tuple-element.14.gin_ref, ...), custom_call_target="tpu_custom_call" | custom-call | tf_op jit(solution)/shard_map/pallas_call | solution.py:532

commit v3 on v2

v3 whole, which is shorter than its diff:
```python
import functools
import math

import jax
import jax.numpy as jnp
from jax import lax
from jax.experimental import pallas as pl
from jax.experimental.pallas import tpu as pltpu
from jax.sharding import PartitionSpec as P

MESH = pl.DeviceIdType.MESH
F32 = jnp.float32
BF16 = jnp.bfloat16
PAD = 8
XROWS = 4
GROWS = 2
GROUPS = 4


def triple(field, forward):
    count = field.shape[0]
    before = pltpu.roll(field, 1, 0).astype(BF16)
    after = pltpu.roll(field, count - 1, 0).astype(BF16)
    if forward:
        return before, field.astype(BF16), after
    return after, field.astype(BF16), before


def gate(value):
    return 0.5 * jnp.tanh(0.5 * value) + 0.5


def slope(sig, act):
    return sig * (1.0 - act) + act


def kernel(sizes, x_hbm, w_hbm, b_hbm, g_hbm,
           wout, bout, gin, skip,
           xpad, gpad, b_ref, wv, wt,
           x3, a3, g3, p3, s1,
           part, rc, m1, rl, mid, rn, bpart, bmid,
           pool32, pool, skip_in,
           local_sem, halo_recv, red_recv, sent_sem):
    nseg, L, N, H, W, C, S, used, scale, G = sizes
    WP, L2 = W + 2 * PAD, L // 2
    seg, lat, lon = lax.axis_index("segment"), lax.axis_index("lat"), lax.axis_index("lon")

    loads = [
        pltpu.make_async_copy(w_hbm, wv, local_sem.at[0]),
        pltpu.make_async_copy(x_hbm, xpad.at[pl.ds(XROWS, H), pl.ds(PAD, W)], local_sem.at[1]),
        pltpu.make_async_copy(g_hbm, gpad.at[pl.ds(GROWS, H), pl.ds(PAD, W)], local_sem.at[2]),
        pltpu.make_async_copy(b_hbm, b_ref, local_sem.at[3]),
    ]
    for load in loads:
        load.start()

    def lat_peer(d):
        return lax.rem(lat + d, L)

    def lon_peer(d):
        return lax.rem(lon + (d + N), N)

    barrier = pltpu.get_barrier_semaphore()

    def greet(s, a, o):
        pl.semaphore_signal(barrier, inc=1, device_id=(s, a, o), device_id_type=MESH)

    for d in range(1, L):
        greet(seg, lat_peer(d), lon)
    for d in range(1, N):
        greet(seg, lat, lon_peer(d))

    @pl.when(lat > 0)
    def _():
        greet(seg, lat - 1, lon_peer(1))
        greet(seg, lat - 1, lon_peer(-1))

    @pl.when(lat < L - 1)
    def _():
        greet(seg, lat + 1, lon_peer(1))
        greet(seg, lat + 1, lon_peer(-1))

    @pl.when(seg > 0)
    def _():
        greet(seg - 1, lat, lon)

    @pl.when(seg < nseg - 1)
    def _():
        greet(seg + 1, lat, lon)

    def flag(condition):
        return lax.convert_element_type(condition, jnp.int32)

    peers = (L - 1 + N - 1 + 2 * flag(lat > 0) + 2 * flag(lat < L - 1)
             + flag(seg > 0) + flag(seg < nseg - 1))
    pl.semaphore_wait(barrier, peers)

    low = 2 * lon < N
    far = jnp.where(low, -1, 1)

    def halo_copy(which, dl, turn):
        ref, dst, rows = (x_hbm, xpad, XROWS) if which == 0 else (g_hbm, gpad, GROWS)
        r = {1: pl.ds(H - rows, rows), -1: pl.ds(0, rows), 0: pl.ds(0, H)}[dl]
        to_r = {1: pl.ds(0, rows), -1: pl.ds(rows + H, rows), 0: pl.ds(rows, H)}[dl]
        do = turn * far
        if turn == 0:
            c, to_c = pl.ds(0, W), pl.ds(PAD, W)
        else:
            c = pl.ds(pl.multiple_of(jnp.where(do > 0, W - PAD, 0), PAD), PAD)
            to_c = pl.ds(pl.multiple_of(jnp.where(do > 0, 0, W + PAD), PAD), PAD)
        return pltpu.make_async_remote_copy(
            src_ref=ref.at[r, c],
            dst_ref=dst.at[to_r, to_c],
            send_sem=sent_sem.at[0],
            recv_sem=halo_recv.at[which, dl % 3],
            device_id=(seg, lat + dl, lon_peer(do)),
            device_id_type=MESH,
        )

    def start_halo(which):
        for turn in (1, 0, -1):
            for dl in (1, -1, 0):
                if dl == 0:
                    if turn:
                        halo_copy(which, dl, turn).start()
                else:
                    @pl.when((lat < L - 1) if dl == 1 else (lat > 0))
                    def _():
                        halo_copy(which, dl, turn).start()

    def halo_whole(which, dl):
        dst, rows = (xpad, XROWS) if which == 0 else (gpad, GROWS)
        if dl == 0:
            region = dst.at[pl.ds(rows, H), pl.ds(0, 2 * PAD)]
        else:
            region = dst.at[pl.ds(0 if dl == 1 else rows + H, rows)]
        return pltpu.make_async_remote_copy(
            src_ref=region, dst_ref=region, send_sem=sent_sem.at[0], recv_sem=halo_recv.at[which, dl % 3],
            device_id=(seg, lat, lon_peer(1)), device_id_type=MESH)

    def recv_halo(which):
        @pl.when(lat > 0)
        def _():
            halo_whole(which, 1).wait_recv()

        @pl.when(lat < L - 1)
        def _():
            halo_whole(which, -1).wait_recv()
        halo_whole(which, 0).wait_recv()

    def sent_halo(which):
        @pl.when(lat < L - 1)
        def _():
            halo_whole(which, 1).wait_send()

        @pl.when(lat > 0)
        def _():
            halo_whole(which, -1).wait_send()
        halo_whole(which, 0).wait_send()

    start_halo(0)
    start_halo(1)

    @pl.when(lat == 0)
    def _():
        xpad[0:XROWS] = jnp.zeros((XROWS, WP, C), BF16)
        gpad[0:GROWS] = jnp.zeros((GROWS, WP, C), BF16)

    @pl.when(lat == L - 1)
    def _():
        xpad[XROWS + H:] = jnp.zeros((XROWS, WP, C), BF16)
        gpad[GROWS + H:] = jnp.zeros((GROWS, WP, C), BF16)

    loads[0].wait()
    for ly in range(2):
        for k in range(9):
            wt[ly, k * C:(k + 1) * C, :] = wv[ly, k * C:(k + 1) * C, :].T
    loads[1].wait()
    loads[2].wait()
    loads[3].wait()
    recv_halo(0)

    def put(ref, field, forward):
        for q, part_ in enumerate(triple(field, forward)):
            ref[:, q * C:(q + 1) * C] = part_

    def window(ref, starts, rows):
        return jnp.concatenate([ref[s * WP:(s + rows) * WP, :] for s in starts], axis=1)

    def clear(ref, first, rows, total):
        @pl.when(lat == 0)
        def _():
            ref[0:rows * WP, :] = jnp.zeros((rows * WP, 3 * C), BF16)

        @pl.when(lat == L - 1)
        def _():
            ref[(total - rows) * WP:total * WP, :] = jnp.zeros((rows * WP, 3 * C), BF16)

    put(x3, xpad[...].astype(F32).reshape((H + 2 * XROWS) * WP, C), True)
    R1, R2, R3 = H + 6, H + 4, H + 2
    z1 = jnp.dot(window(x3, (0, 1, 2), R1), wv[0], preferred_element_type=F32) + b_ref[0:1, :]
    sig = gate(z1)
    a1 = z1 * sig
    s1[...] = slope(sig, a1)[2 * WP:(2 + R3) * WP, :]
    put(a3, a1, True)
    clear(a3, 0, 3, R1)

    recv_halo(1)
    z2 = jnp.dot(window(a3, (0, 1, 2), R2), wv[1], preferred_element_type=F32) + b_ref[1:2, :]
    up = gpad[...].astype(F32).reshape((H + 2 * GROWS) * WP, C)
    sig = gate(z2)
    g2 = up * slope(sig, z2 * sig)
    put(g3, g2, False)

    column = lax.rem(lax.broadcasted_iota(jnp.int32, (H * WP, C), 0), WP)
    inside = (column >= PAD) & (column < PAD + W)

    def grads(field, start, first, ly, brow):
        own = jnp.where(inside, field[first * WP:(first + H) * WP, :].astype(BF16).astype(F32), 0.0)
        bsum = jnp.sum(own, axis=0, keepdims=True)
        bpart[lat, brow * 8:brow * 8 + 8, :] = jnp.broadcast_to(bsum, (8, C))
        flipped = own.astype(BF16).T
        ref = a3 if ly else x3
        for p in range(3):
            block = ref[(start + p) * WP:(start + p + H) * WP, :]
            three = jnp.dot(flipped, block, preferred_element_type=F32).astype(BF16)
            for q in range(3):
                yield three[:, q * C:(q + 1) * C].T

    def store_part(ly, blocks):
        whole = jnp.concatenate([v.astype(F32) for v in blocks], axis=0)
        extra = used * S - whole.shape[0]
        if extra:
            whole = jnp.concatenate([whole, jnp.zeros((extra, C), F32)], axis=0)
        for i in range(L * N):
            value = whole[i * S:(i + 1) * S].astype(BF16) if i < used else jnp.zeros((S, C), BF16)
            part[ly, i // (L2 * N), i // N % L2, i % N] = value

    core, y = lax.rem(lat, 2), lat // 2
    partner = (2 * y + 1 - core, lon)
    Z = N // G
    own = lon // Z
    mirrored = jnp.where(low, own, G - 1 - own)
    CRS, ZRS, YAG, CAG, YRS = 0, 1, 2, 3, 4
    ZAG = YRS + G
    pending = []

    def copy_to(src, dst, at, ly, peer):
        return pltpu.make_async_remote_copy(
            src_ref=src, dst_ref=dst, send_sem=sent_sem.at[0], recv_sem=red_recv.at[ly, at],
            device_id=(seg,) + peer, device_id_type=MESH)

    def arrived(region, at, ly):
        copy_to(region, region, at, ly, partner).wait_recv()

    def send(src, dst, at, ly, peer):
        copy_to(src, dst, at, ly, peer).start()
        pending.append(src)

    def near(k):
        if k == 0:
            return own
        at = k - 1 + jnp.where(k - 1 >= mirrored, 1, 0)
        return jnp.where(low, at, G - 1 - at)

    def zs(k):
        return pl.ds(near(k) * Z, Z)

    def y_to(d):
        return lax.rem(y + d, L2)

    def y_peer(d):
        return (2 * y_to(d) + core, lon)

    def rs_core(ly):
        send(part.at[ly, 1 - core], rc.at[ly], CRS, ly, partner)

    def rs_y(ly):
        arrived(rc.at[ly], CRS, ly)
        for k in reversed(range(G)):
            m1[ly, :, zs(k)] = (part[ly, core, :, zs(k)].astype(F32) + rc[ly, :, zs(k)].astype(F32)).astype(BF16)
            for d in range(1, L2):
                send(m1.at[ly, y_to(d), zs(k)], rl.at[ly, d - 1, zs(k)], YRS + k, ly, y_peer(d))

    def z_away(k, act):
        for j in reversed(range(Z)):
            t = near(k) * Z + j

            @pl.when(t != lon)
            def _():
                act(t, lax.rem(t - lon + N, N))

    def rs_z(ly, k):
        total = m1[ly, y, zs(k)].astype(F32)
        if L2 > 1:
            arrived(rl.at[ly, :, zs(k)], YRS + k, ly)
        for d in range(1, L2):
            total = total + rl[ly, L2 - d - 1, zs(k)].astype(F32)
        mid[ly, zs(k)] = total.astype(BF16)
        z_away(k, lambda t, d: copy_to(mid.at[ly, t], rn.at[ly, d - 1], ZRS, ly, (lat, t)).start())

    def total_z(ly):
        total = mid[ly, lon].astype(F32)
        arrived(rn.at[ly], ZRS, ly)
        for d in range(1, N):
            total = total + rn[ly, N - d - 1].astype(F32)
        wout[ly, core, y, lon] = (total * scale).astype(BF16)
        piece = wout.at[ly, core, y, lon]
        for k in reversed(range(G)):
            z_away(k, lambda t, d: copy_to(piece, piece, ZAG + d - 1, ly, (lat, t)).start())

    def forward(ly, k):
        for j in range(Z):
            frm = near(k) * Z + j

            @pl.when(frm != lon)
            def _():
                arrived(wout.at[ly, core, y, frm], ZAG + lax.rem(lon - frm + N, N) - 1, ly)

        piece = wout.at[ly, core, y, zs(k)]
        for d in range(1, L2):
            send(piece, piece, YAG, ly, y_peer(d))
        send(piece, piece, CAG, ly, partner)

    def forward_y(ly):
        for d in range(1, L2):
            arrived(wout.at[ly, core, y], YAG, ly)
        for d in range(1, L2):
            piece = wout.at[ly, core, y_to(d)]
            send(piece, piece, CAG, ly, partner)

    def settle(ly):
        arrived(wout.at[ly, 1 - core], CAG, ly)

    store_part(1, grads(g2, 2, 2, 1, 1))
    rs_core(1)

    h1 = lax.dot_general(window(g3, (2, 1, 0), R3), wt[1], (((1,), (0,)), ((), ())),
                         preferred_element_type=F32)
    g1 = h1 * s1[...]
    put(p3, g1, False)
    clear(p3, 0, 1, R3)
    rs_y(1)

    store_part(0, grads(g1, 3, 1, 0, 0))
    rs_core(0)
    for d in range(1, L):
        send(bpart.at[lat], bpart.at[lat], 0, 2, (lat_peer(d), lon))

    gi = jnp.dot(window(p3, (2, 1, 0), H), wt[0], preferred_element_type=F32)
    gi = gi.reshape(H, WP, C)[:, PAD:PAD + W, :]
    gin[...] = gi.astype(BF16)
    rows = gi.reshape(H // 2, 2, W, C)
    pool32[...] = (rows[:, 0] + rows[:, 1]).reshape(H // 2 * W, C)
    half = H // 2 * W // 2
    pool[...] = (pool32[pl.ds(0, half, stride=2), :] + pool32[pl.ds(1, half, stride=2), :]).astype(BF16)

    def skip_copy(to):
        return pltpu.make_async_remote_copy(
            src_ref=pool, dst_ref=skip_in, send_sem=sent_sem.at[0], recv_sem=red_recv.at[2, 2],
            device_id=(to, lat, lon), device_id_type=MESH)

    rs_y(0)

    @pl.when(seg > 0)
    def _():
        skip_copy(seg - 1).start()

    for k in reversed(range(G)):
        rs_z(1, k)
    arrived(bpart.at[pl.ds(0, L - 1)], 0, 2)
    total = bpart[0]
    for i in range(1, L):
        total = total + bpart[i]
    bmid[lon] = total
    for d in range(1, N):
        send(bmid.at[lon], bmid.at[lon], 1, 2, (lat, lon_peer(d)))
    for k in reversed(range(G)):
        rs_z(0, k)
    total_z(1)
    forward(1, 0)
    total_z(0)
    forward(0, 0)
    for k in range(1, G):
        forward(1, k)
    for k in range(1, G):
        forward(0, k)
    forward_y(1)
    arrived(bmid.at[pl.ds(0, N - 1)], 1, 2)
    total = bmid[0]
    for i in range(1, N):
        total = total + bmid[i]
    bout[...] = jnp.concatenate([total[0:1], total[8:9]], axis=0) * scale

    @pl.when(seg < nseg - 1)
    def _():
        skip_copy(seg).wait_recv()
        skip[...] = skip_in[...]

    @pl.when(seg == nseg - 1)
    def _():
        skip[...] = jnp.zeros(skip.shape, BF16)

    forward_y(0)
    settle(1)
    settle(0)
    for src in pending:
        copy_to(src, src, 0, 2, partner).wait_send()
    for ly in range(2):
        for ref in (mid, wout.at[:, core, y]):
            src = ref.at[ly, pl.ds(0, N - 1)]
            copy_to(src, src, 0, 2, partner).wait_send()
    sent_halo(0)
    sent_halo(1)

    @pl.when(seg > 0)
    def _():
        skip_copy(seg - 1).wait_send()


def finish(rows, w_ref, b_ref, gin_ref, skip_ref, w_out, b_out, gin_out, skip_out, wide, sem):
    copies = [pltpu.make_async_copy(gin_ref, gin_out, sem.at[0]),
              pltpu.make_async_copy(b_ref, b_out, sem.at[1]),
              pltpu.make_async_copy(skip_ref, skip_out, sem.at[2])]
    for copy in copies:
        copy.start()
    for ly in range(2):
        flat = w_ref[ly].reshape(-1, w_ref.shape[-1])
        wide[ly] = flat[:rows].astype(F32)
        copy = pltpu.make_async_copy(wide.at[ly], w_out.at[ly], sem.at[3 + ly])
        copy.start()
        copies.append(copy)
    for copy in copies:
        copy.wait()


def body(mesh_sizes, segment_input, weights, biases, out_grad):
    nseg, L, N = mesh_sizes
    _, H, W, C = segment_input.shape
    total_rows = 9 * C
    S = 8 * (-(-total_rows // (8 * L * N)))
    used = -(-total_rows // S)
    scale = 1.0 / math.sqrt(H * L * W * N)
    WP = W + 2 * PAD
    G = math.gcd(N, GROUPS)
    sizes = (nseg, L, N, H, W, C, S, used, scale, G)
    VM = pltpu.VMEM
    dma = pltpu.SemaphoreType.DMA
    per = 4 + G + N - 1
    vmem = pl.BlockSpec(memory_space=pltpu.VMEM)
    anyspace = pl.BlockSpec(memory_space=pl.ANY)
    hbm = pl.BlockSpec(memory_space=pltpu.HBM)
    half = H // 2 * W // 2
    finish_bytes = 2 * total_rows * C * 4 + (1 << 20)

    def in_hbm(array):
        return pltpu.with_memory_space_constraint(array, pltpu.HBM)

    wout, bout, gin, skip = pl.pallas_call(
        functools.partial(kernel, sizes),
        out_shape=(
            VM((2, 2, L // 2, N, S, C), BF16),
            VM((2, C), F32),
            VM((H, W, C), BF16),
            VM((half, C), BF16),
        ),
        in_specs=[hbm, hbm, hbm, hbm],
        out_specs=(vmem, vmem, vmem, vmem),
        scratch_shapes=[
            VM((H + 2 * XROWS, WP, C), BF16), VM((H + 2 * GROWS, WP, C), BF16), VM((2, C), F32),
            VM((2, 9 * C, C), BF16), VM((2, 9 * C, C), BF16),
            VM(((H + 8) * WP, 3 * C), BF16), VM(((H + 6) * WP, 3 * C), BF16),
            VM(((H + 4) * WP, 3 * C), BF16), VM(((H + 2) * WP, 3 * C), BF16),
            VM(((H + 2) * WP, C), F32),
            VM((2, 2, L // 2, N, S, C), BF16), VM((2, L // 2, N, S, C), BF16), VM((2, L // 2, N, S, C), BF16),
            VM((2, L // 2 - 1, N, S, C), BF16), VM((2, N, S, C), BF16), VM((2, N - 1, S, C), BF16),
            VM((L, 16, C), F32), VM((N, 16, C), F32),
            VM((H // 2 * W, C), F32), VM((H // 2 * W // 2, C), BF16), VM((H // 2 * W // 2, C), BF16),
            dma((4,)), dma((2, 3)), dma((3, per)), dma((1,)),
        ],
        compiler_params=pltpu.CompilerParams(collective_id=0, has_side_effects=True,
                                             vmem_limit_bytes=48 << 20),
    )(in_hbm(segment_input[0]), in_hbm(weights[0].reshape(2, 9 * C, C)), in_hbm(biases[0]), in_hbm(out_grad[0]))
    weight_grad, bias_grad, gin, skip = pl.pallas_call(
        functools.partial(finish, total_rows),
        out_shape=(
            jax.ShapeDtypeStruct((2, total_rows, C), F32),
            jax.ShapeDtypeStruct((2, C), F32),
            jax.ShapeDtypeStruct((H, W, C), BF16),
            jax.ShapeDtypeStruct((half, C), BF16),
        ),
        in_specs=[vmem] * 4,
        out_specs=(anyspace,) * 4,
        scratch_shapes=[VM((2, total_rows, C), F32), dma((5,))],
        compiler_params=pltpu.CompilerParams(vmem_limit_bytes=finish_bytes),
    )(wout, bout, gin, skip)
    return (weight_grad.reshape(1, 2, 3, 3, C, C), bias_grad[None], gin[None],
            skip.reshape(1, H // 2, W // 2, C))


def solution(mesh):
    placed = (
        P("segment", "lat", "lon", None),
        P("segment", None, None, None, None, None),
        P("segment", None, None),
        P("segment", "lat", "lon", None),
    )
    mesh_sizes = (mesh.shape["segment"], mesh.shape["lat"], mesh.shape["lon"])
    return jax.shard_map(
        functools.partial(body, mesh_sizes),
        mesh=mesh,
        in_specs=placed,
        out_specs=(
            P("segment", None, None, None, None, None),
            P("segment", None, None),
            P("segment", "lat", "lon", None),
            P("segment", "lat", "lon", None),
        ),
        check_vma=False,
    )
```

time: 36 us -> 32.8 us (0.911)
  Pallas kernels: 35.2 us -> 32 us
    pallas_call x1, Pallas kernels: 34.1 us -> 30.9 us  [body(): pl.pallas_call(functools.partial(kernel, sizes), out_shape=(VM((2, 2, L /...]
where the time goes in v3:
time: 32.8 us; the launch traced here: 32.6 us
  Pallas kernels  32 us (98%)
  between operations  0.64 us (2%)
    pallas_call x1, Pallas kernels, body(): pl.pallas_call(functools.partial(kernel, sizes), out_shape=(VM((2, 2, L /...  30.9 us
    pallas_call x1, Pallas kernels, body(): pl.pallas_call(functools.partial(finish, total_rows), out_shape=(jax.Shap...  1.11 us

profile of v3, /device:TPU:0, one launch (start us, length us, event | category | flops | bytes accessed | tf_op | source)
XLA Modules:
  0.0 32.6 jit_solution(14487030402113301916)
XLA Ops:
  0.6 30.9 %shard_map.75 = (bf16[2,2,2,4,72,128]{5,4,3,2,1,0:T(8,128)(2,1)S(1)}, f32[2,128]{1,0:T(2,128)S(1)}, bf16[8,64,128]{2,1,0:T(8,128)(2,1)S(1)}, bf16[128,128]{1,0:T(8,128)(2,1)S(1)}) custom-call(bf16[8,64,128]{2,1,0:T(8,128)(2,1)} %bitcast.9, bf16[2,1152,128]{2,1,0:T(8,128)(2,1)} %bitcast.8, f32[2,128]{1,0:T(2,128)} %bitcast.11, bf16[8,64,128]{2,1,0:T(8,128)(2,1)} %bitcast.10), custom_call_target="tpu_custom_call" | custom-call | tf_op jit(solution)/shard_map/pallas_call | solution.py:459
  31.5 1.1 %shard_map.76 = (f32[2,1152,128]{2,1,0:T(8,128)}, f32[2,128]{1,0:T(2,128)}, bf16[8,64,128]{2,1,0:T(8,128)(2,1)}, bf16[128,128]{1,0:T(8,128)(2,1)}) custom-call(bf16[2,2,2,4,72,128]{5,4,3,2,1,0:T(8,128)(2,1)S(1)} %get-tuple-element.12.w_ref, f32[2,128]{1,0:T(2,128)S(1)} %get-tuple-element.13.b_ref, bf16[8,64,128]{2,1,0:T(8,128)(2,1)S(1)} %get-tuple-element.14.gin_ref, ...), custom_call_target="tpu_custom_call" | custom-call | tf_op jit(solution)/shard_map/pallas_call | solution.py:484
